TPU v7x, 32 devices: a whole 2x2x4 slice. The times are simulated.
32 devices in a mesh: head: 8 (over z, y), dp: 4 (over x, core).
Axes of the slice: x: 2, y: 2, z: 4, core: 2. Of those that a mesh axis runs over, the one named last changes fastest.
Arguments:
- attn_out: bfloat16 [1024, 8192], P('dp', 'head'), may hold values from -6 to 6
- head_mask: int32 [64], P('head'), may hold values from 0 to 1, as said below
- gate_scale: float32 [64], P('head'), may hold values from 0.25 to 2
- w_out: bfloat16 [8192, 8192], P('head', 'dp'), may hold values from -0.09375 to 0.09375
- grad_out: bfloat16 [1024, 8192], P(('dp', 'head')), may hold values from -6 to 6
Outputs:
- proj_out: bfloat16 [1024, 8192], P(('dp', 'head'))
- grad_attn: bfloat16 [1024, 8192], P('dp', 'head')
- grad_w: float32 [8192, 8192], P('head', 'dp')
Inputs may be any that keep to these rules, and one draw needn't show every extreme that they name: `head_mask`: exactly 32 heads are live.
All inputs are finite; a program needn't handle non-finite values.
Results may differ from a plain program's by a relative error of at most 0.0051.
Values may be sent and summed in bfloat16 or wider, within the bound.
A program may use at most 128 MiB of HBM per device.

v0:
```python
import jax
import jax.numpy as jnp
from jax import lax
from jax.sharding import PartitionSpec as P


def shards(attn_out, head_mask, gate_scale, w_out, grad_out):
    gate_vals = head_mask.astype(jnp.float32) * gate_scale
    width_each = attn_out.shape[1] // gate_vals.shape[0]
    col_gate = jnp.repeat(gate_vals, width_each)
    gated = (attn_out.astype(jnp.float32) * col_gate[None, :]).astype(jnp.bfloat16)
    weight_rows = lax.all_gather(w_out, "dp", axis=1, tiled=True)
    proj_out = lax.psum_scatter(
        jnp.dot(gated, weight_rows, preferred_element_type=jnp.float32),
        "head",
        scatter_dimension=0,
        tiled=True,
    ).astype(jnp.bfloat16)
    grad_full = lax.all_gather(grad_out, "head", axis=0, tiled=True)
    back_proj = lax.dot_general(
        grad_full, weight_rows, (((1,), (1,)), ((), ())), preferred_element_type=jnp.float32
    )
    grad_attn = (back_proj * col_gate[None, :]).astype(jnp.bfloat16)
    grad_local = lax.dot_general(
        gated, grad_full, (((0,), (0,)), ((), ())), preferred_element_type=jnp.float32
    )
    grad_w = lax.psum_scatter(grad_local, "dp", scatter_dimension=1, tiled=True)
    return (proj_out, grad_attn, grad_w)


def solution(mesh):
    return jax.shard_map(
        shards,
        mesh=mesh,
        in_specs=(P("dp", "head"), P("head"), P("head"), P("head", "dp"), P(("dp", "head"), None)),
        out_specs=(P(("dp", "head"), None), P("dp", "head"), P("head", "dp")),
        check_vma=False,
    )
```

profile of v0, /device:TPU:0, one launch (start us, length us, event | category | flops | bytes accessed | tf_op | source)
XLA Modules:
  0.0 583.7 jit_solution(12137804477661444461)
XLA Ops:
  7.2 0.0 all-gather.3.cloned.1.call-start
  7.2 0.7 all-gather.3.cloned.1.call-update
  7.9 0.0 all-gather.5.cloned.1.call-start
  7.9 0.7 all-gather.5.cloned.1.call-update
  8.6 0.0 reduce-scatter.3.cloned.1.call-start
  8.7 0.7 convert_multiply_fusion
  9.4 0.1 broadcast_bitcast_fusion
  9.4 108.7 %all-gather.3.cloned.1.call-done = bf16[1024,8192]{1,0:T(8,128)(2,1)} async-done(((bf16[1024,2048]{1,0:T(8,128)(2,1)}), bf16[1024,8192]{1,0:T(8,128)(2,1)}) %all-gather.3.cloned.1.call-update) | async-done | bytes 16777232 | tf_op jit(solution)/shard_map/all_gather | solution.py:12
  118.2 13.7 %fusion.2 = f32[256,8192]{1,0:T(8,128)} fusion(bf16[1024,8192]{1,0:T(8,128)(2,1)} %all-gather.3.cloned.1.call-done, bf16[256,1024]{1,0:T(8,128)(2,1)} %param.5, f32[1024]{0:T(1024)S(1)} %broadcast_bitcast_fusion), kind=kOutput, calls=%fused_computation.4 | convolution fusion | flops 4295753728 | bytes 25694208 | tf_op jit(solution)/shard_map/dot_general | solution.py:14
  131.9 0.0 copy-start
  131.9 0.0 reduce-scatter.3.cloned.1.call-update
  131.9 0.0 reduce-scatter.5.cloned.1.call-start
  131.9 61.2 %all-gather.5.cloned.1.call-done = bf16[256,8192]{1,0:T(8,128)(2,1)} async-done(((bf16[32,8192]{1,0:T(8,128)(2,1)}), bf16[256,8192]{1,0:T(8,128)(2,1)}) %all-gather.5.cloned.1.call-update) | async-done | bytes 4194320 | tf_op jit(solution)/shard_map/all_gather | solution.py:19
  193.1 0.0 copy-done
  193.1 15.9 %fusion.1 = f32[1024,8192]{1,0:T(8,128)} fusion(bf16[256,8192]{1,0:T(8,128)(2,1)} %all-gather.5.cloned.1.call-done, bf16[256,1024]{1,0:T(8,128)(2,1)S(1)} %copy-done, f32[1024]{0:T(1024)S(1)} %broadcast_bitcast_fusion), kind=kOutput, calls=%fused_computation.3 | convolution fusion | flops 4295753728 | bytes 38277120 | tf_op jit(solution)/shard_map/dot_general | solution.py:24
  209.0 0.0 reduce-scatter.5.cloned.1.call-update
  209.1 12.5 %fusion = bf16[256,1024]{1,0:T(8,128)(2,1)} fusion(bf16[256,8192]{1,0:T(8,128)(2,1)} %all-gather.5.cloned.1.call-done, bf16[1024,8192]{1,0:T(8,128)(2,1)} %all-gather.3.cloned.1.call-done, f32[1024]{0:T(1024)S(1)} %broadcast_bitcast_fusion), kind=kOutput, calls=%fused_computation.1 | convolution fusion | flops 4295491584 | bytes 21499904 | tf_op jit(solution)/shard_map/dot_general | solution.py:20
  221.5 121.3 %reduce-scatter.3.cloned.1.call-done = f32[32,8192]{1,0:T(8,128)} async-done(((f32[256,8192]{1,0:T(8,128)}), f32[32,8192]{1,0:T(8,128)}) %reduce-scatter.3.cloned.1.call-update) | async-done | bytes 1048592 | tf_op jit(solution)/shard_map/reduce_scatter | solution.py:13
  342.8 2.1 convert_element_type.18
  344.9 232.3 %reduce-scatter.5.cloned.1.call-done = f32[1024,2048]{1,0:T(8,128)} async-done(((f32[1024,8192]{1,0:T(8,128)}), f32[1024,2048]{1,0:T(8,128)}) %reduce-scatter.5.cloned.1.call-update) | async-done | bytes 8388624 | tf_op jit(solution)/shard_map/reduce_scatter | solution.py:27
Async XLA Ops:
  7.2 111.0 %all-gather.3.cloned.1.call-start = ((), (), s32[]{:S(2)}) async-start(), calls=%async_computation.2 | async-start | bytes 20971520 | tf_op jit(solution)/shard_map/all_gather | solution.py:12
  7.9 185.2 %all-gather.5.cloned.1.call-start = ((), (), s32[]{:S(2)}) async-start(), calls=%async_computation.4 | async-start | bytes 4718592 | tf_op jit(solution)/shard_map/all_gather | solution.py:19
  8.6 334.2 %reduce-scatter.3.cloned.1.call-start = ((), (), s32[]{:S(2)}) async-start(), calls=%async_computation.3 | async-start | bytes 9437184 | tf_op jit(solution)/shard_map/reduce_scatter | solution.py:13
  131.9 61.3 %copy-start = (bf16[256,1024]{1,0:T(8,128)(2,1)S(1)}, bf16[256,1024]{1,0:T(8,128)(2,1)}, u32[]{:S(2)}) copy-start(bf16[256,1024]{1,0:T(8,128)(2,1)} %param.5) | copy-start | bytes 1572868
  131.9 445.3 %reduce-scatter.5.cloned.1.call-start = ((), (), s32[]{:S(2)}) async-start(), calls=%async_computation.5 | async-start | bytes 41943040 | tf_op jit(solution)/shard_map/reduce_scatter | solution.py:27
Sparse Core Ops, SparseCore 0:
  9.5 108.6 all-gather.2
  120.3 72.7 all-gather.4
  196.8 145.9 reduce-scatter.2
  345.8 231.3 reduce-scatter.4
where the time goes:
time: 584 us
  waiting for transfers between devices  525 us (90%)
  matrix products  42.1 us (7%)
  between operations  13.8 us (2%)
    reduce_scatter x1, waiting for transfers between devices, shards(): grad_w = lax.psum_scatter(grad_local, 'dp', scatter_dimension=1, tiled=True)  232 us
    reduce_scatter x1, waiting for transfers between devices, shards(): lax.psum_scatter(jnp.dot(gated, weight_rows, preferred_element_type=jnp.f...  121 us
    all_gather x1, waiting for transfers between devices, shards(): weight_rows = lax.all_gather(w_out, 'dp', axis=1, tiled=True)  109 us
    all_gather x1, waiting for transfers between devices, shards(): grad_full = lax.all_gather(grad_out, 'head', axis=0, tiled=True)  61.2 us
    dot_general x1, matrix products, shards(): lax.dot_general(gated, grad_full, (((0,), (0,)), ((), ())), preferred_ele...  15.9 us
    dot_general x1, matrix products, shards(): jnp.dot(gated, weight_rows, preferred_element_type=jnp.float32)  13.7 us
    dot_general x1, matrix products, shards(): lax.dot_general(grad_full, weight_rows, (((1,), (1,)), ((), ())), preferr...  12.5 us
  transfers between devices with their start and end apart: 4, of which 4 were waited for; matrix products, arithmetic and copies ran while one was open for 8% of the time, Pallas kernels for 0%

commit v1 on v0

--- a/solution.py
+++ b/solution.py
@@ -9,7 +9,7 @@
     width_each = attn_out.shape[1] // gate_vals.shape[0]
     col_gate = jnp.repeat(gate_vals, width_each)
     gated = (attn_out.astype(jnp.float32) * col_gate[None, :]).astype(jnp.bfloat16)
-    weight_rows = lax.all_gather(w_out, "dp", axis=1, tiled=True)
+    weight_rows = jnp.concatenate(lax.all_gather(w_out, "dp"), 1)
     proj_out = lax.psum_scatter(
         jnp.dot(gated, weight_rows, preferred_element_type=jnp.float32),
         "head",

time: 584 us -> 584 us (level)
  waiting for transfers between devices: 525 us -> 497 us
  local copies, waits for them, and re-layouts: 0.08 us -> 22.7 us
    all_gather x1, waiting for transfers between devices: 61.2 us -> 33.1 us  [shards(): grad_full = lax.all_gather(grad_out, 'head', axis=0, tiled=True)]
    reshape x0 -> x1, local copies, waits for them, and re-layouts: none -> 22.7 us  [shards(): weight_rows = jnp.concatenate(lax.all_gather(w_out, 'dp'), 1)]
  transfers between devices with their start and end apart: 4 -> 4, of which waited for: 4 -> 4; matrix products, arithmetic and copies ran while one was open for 8% -> 12% of each run, Pallas kernels for 0% -> 0%
where the time goes in v1:
time: 584 us
  waiting for transfers between devices  497 us (85%)
  matrix products  47.5 us (8%)
  local copies, waits for them, and re-layouts  22.7 us (4%)
  between operations  13.8 us (2%)
    reduce_scatter x1, waiting for transfers between devices, shards(): grad_w = lax.psum_scatter(grad_local, 'dp', scatter_dimension=1, tiled=True)  232 us
    reduce_scatter x1, waiting for transfers between devices, shards(): lax.psum_scatter(jnp.dot(gated, weight_rows, preferred_element_type=jnp.f...  121 us
    all_gather x1, waiting for transfers between devices, shards(): weight_rows = jnp.concatenate(lax.all_gather(w_out, 'dp'), 1)  109 us
    all_gather x1, waiting for transfers between devices, shards(): grad_full = lax.all_gather(grad_out, 'head', axis=0, tiled=True)  33.1 us
    reshape x1, local copies, waits for them, and re-layouts, shards(): weight_rows = jnp.concatenate(lax.all_gather(w_out, 'dp'), 1)  22.7 us
    dot_general x1, matrix products, shards(): jnp.dot(gated, weight_rows, preferred_element_type=jnp.float32)  19.1 us
    dot_general x1, matrix products, shards(): lax.dot_general(gated, grad_full, (((0,), (0,)), ((), ())), preferred_ele...  15.9 us
    dot_general x1, matrix products, shards(): lax.dot_general(grad_full, weight_rows, (((1,), (1,)), ((), ())), preferr...  12.4 us
  transfers between devices with their start and end apart: 4, of which 4 were waited for; matrix products, arithmetic and copies ran while one was open for 12% of the time, Pallas kernels for 0%

profile of v1, /device:TPU:0, one launch (start us, length us, event | category | flops | bytes accessed | tf_op | source)
XLA Modules:
  0.0 583.7 jit_solution(817551873693366502)
XLA Ops:
  7.2 0.0 all-gather.6.cloned.1.call-start
  7.2 0.7 all-gather.6.cloned.1.call-update
  7.9 0.0 all-gather.4.cloned.1.call-start
  7.9 0.7 all-gather.4.cloned.1.call-update
  8.6 0.0 reduce-scatter.3.cloned.1.call-start
  8.7 0.7 convert_multiply_fusion
  9.4 0.1 broadcast_bitcast_fusion
  9.4 108.7 %all-gather.6.cloned.1.call-done = bf16[4096,2048]{1,0:T(8,128)(2,1)} async-done(((bf16[1024,2048]{1,0:T(8,128)(2,1)}), bf16[4096,2048]{1,0:T(8,128)(2,1)}) %all-gather.6.cloned.1.call-update) | async-done | bytes 16777232 | tf_op jit(solution)/shard_map/all_gather | solution.py:12
  118.2 0.0 copy-start
  118.2 22.7 %copy.8 = bf16[1024,4,2048]{0,2,1:T(8,128)(2,1)} copy(bf16[1024,4,2048]{2,0,1:T(8,128)(2,1)} %bitcast.12) | data formatting | bytes 33554432 | tf_op jit(solution)/shard_map/reshape | solution.py:12
  140.8 0.0 copy-done
  140.8 19.1 %fusion.2 = f32[256,8192]{1,0:T(8,128)} fusion(bf16[1024,8192]{0,1:T(8,128)(2,1)} %bitcast.10, bf16[256,1024]{1,0:T(8,128)(2,1)S(1)} %copy-done, f32[1024]{0:T(1024)S(1)} %broadcast_bitcast_fusion), kind=kOutput, calls=%fused_computation.4 | convolution fusion | flops 4295753728 | bytes 25694208 | tf_op jit(solution)/shard_map/dot_general | solution.py:14
  160.0 0.0 reduce-scatter.3.cloned.1.call-update
  160.0 0.0 reduce-scatter.5.cloned.1.call-start
  160.0 33.1 %all-gather.4.cloned.1.call-done = bf16[256,8192]{1,0:T(8,128)(2,1)} async-done(((bf16[32,8192]{1,0:T(8,128)(2,1)}), bf16[256,8192]{1,0:T(8,128)(2,1)}) %all-gather.4.cloned.1.call-update) | async-done | bytes 4194320 | tf_op jit(solution)/shard_map/all_gather | solution.py:19
  193.2 15.9 %fusion.1 = f32[1024,8192]{1,0:T(8,128)} fusion(bf16[256,8192]{1,0:T(8,128)(2,1)} %all-gather.4.cloned.1.call-done, bf16[256,1024]{1,0:T(8,128)(2,1)S(1)} %copy-done, f32[1024]{0:T(1024)S(1)} %broadcast_bitcast_fusion), kind=kOutput, calls=%fused_computation.3 | convolution fusion | flops 4295753728 | bytes 38277120 | tf_op jit(solution)/shard_map/dot_general | solution.py:24
  209.1 0.0 reduce-scatter.5.cloned.1.call-update
  209.1 12.4 %fusion = bf16[256,1024]{1,0:T(8,128)(2,1)} fusion(bf16[256,8192]{1,0:T(8,128)(2,1)} %all-gather.4.cloned.1.call-done, bf16[1024,8192]{0,1:T(8,128)(2,1)} %bitcast.11, f32[1024]{0:T(1024)S(1)} %broadcast_bitcast_fusion), kind=kOutput, calls=%fused_computation.1 | convolution fusion | flops 4295491584 | bytes 21499904 | tf_op jit(solution)/shard_map/dot_general | solution.py:20
  221.5 121.2 %reduce-scatter.3.cloned.1.call-done = f32[32,8192]{1,0:T(8,128)} async-done(((f32[256,8192]{1,0:T(8,128)}), f32[32,8192]{1,0:T(8,128)}) %reduce-scatter.3.cloned.1.call-update) | async-done | bytes 1048592 | tf_op jit(solution)/shard_map/reduce_scatter | solution.py:13
  342.8 2.1 convert_element_type.18
  344.8 232.3 %reduce-scatter.5.cloned.1.call-done = f32[1024,2048]{1,0:T(8,128)} async-done(((f32[1024,8192]{1,0:T(8,128)}), f32[1024,2048]{1,0:T(8,128)}) %reduce-scatter.5.cloned.1.call-update) | async-done | bytes 8388624 | tf_op jit(solution)/shard_map/reduce_scatter | solution.py:27
Async XLA Ops:
  7.2 111.0 %all-gather.6.cloned.1.call-start = ((), (), s32[]{:S(2)}) async-start(), calls=%async_computation.5 | async-start | bytes 20971520 | tf_op jit(solution)/shard_map/all_gather | solution.py:12
  7.9 185.3 %all-gather.4.cloned.1.call-start = ((), (), s32[]{:S(2)}) async-start(), calls=%async_computation.3 | async-start | bytes 4718592 | tf_op jit(solution)/shard_map/all_gather | solution.py:19
  8.6 334.1 %reduce-scatter.3.cloned.1.call-start = ((), (), s32[]{:S(2)}) async-start(), calls=%async_computation.2 | async-start | bytes 9437184 | tf_op jit(solution)/shard_map/reduce_scatter | solution.py:13
  118.2 22.7 %copy-start = (bf16[256,1024]{1,0:T(8,128)(2,1)S(1)}, bf16[256,1024]{1,0:T(8,128)(2,1)}, u32[]{:S(2)}) copy-start(bf16[256,1024]{1,0:T(8,128)(2,1)} %param.5) | copy-start | bytes 1572868
  160.0 417.2 %reduce-scatter.5.cloned.1.call-start = ((), (), s32[]{:S(2)}) async-start(), calls=%async_computation.4 | async-start | bytes 41943040 | tf_op jit(solution)/shard_map/reduce_scatter | solution.py:27
Sparse Core Ops, SparseCore 0:
  9.5 108.6 all-gather.5
  120.3 72.8 all-gather.3
  196.8 145.9 reduce-scatter.2
  345.8 231.3 reduce-scatter.4
